TPU v7x, 32 devices: a whole 2x2x4 slice. The times are simulated.
32 devices in a mesh: band: 4 (over y, core), grid: 8 (over z, x).
Axes of the slice: x: 2, y: 2, z: 4, core: 2. Of those that a mesh axis runs over, the one named last changes fastest.
Arguments:
- orbitals: float32 [64, 16, 4096], P('band', 'grid'), may hold values from -6 to 6
- potential: float32 [16, 4096], P('grid'), may hold values from 0 to 2
Outputs:
- rotated: bfloat16 [64, 16, 4096], P('band', 'grid')
All inputs are finite; a program needn't handle non-finite values. Where the computation divides by a largest or mean magnitude, that divisor is 1e-20 or more.
Results may differ from a plain program's by a relative error of at most 0.001.
The roundings to bfloat16 on the way count: a program that leaves them out, or rounds other values in their place, can miss the bound.
Values may be sent and summed in bfloat16 or wider, within the bound.
A program may use at most 64 MiB of HBM per device.

v0:
```python
import jax
import jax.numpy as jnp
from jax import lax
from jax.sharding import PartitionSpec as P

NX = 64
DEGREE = 2
NS_ITERS = 2


def with_halo(block, sides, width):
    for axis, dim in sides:
        count = lax.axis_size(axis)
        forward = [(i, i + 1) for i in range(count - 1)]
        forward.append((count - 1, 0))
        backward = [(target, source) for source, target in forward]
        low = lax.ppermute(
            lax.slice_in_dim(block, block.shape[dim] - width, None, axis=dim), axis, forward
        )
        high = lax.ppermute(lax.slice_in_dim(block, 0, width, axis=dim), axis, backward)
        block = jnp.concatenate([low, block, high], axis=dim)
    return block


def apply_inner(extended, potential):
    inner = extended[:, 1:-1]
    count = inner.shape[0]
    planes = inner.shape[1]
    square = inner.reshape(count, planes, NX, NX)
    sideways = jnp.roll(square, 1, 2) + jnp.roll(square, -1, 2)
    sideways = sideways + jnp.roll(square, 1, 3) + jnp.roll(square, -1, 3)
    beside = extended[:, 2:] + extended[:, :-2] + sideways.reshape(inner.shape)
    return 0.5 * (6.0 * inner - beside) + potential[None] * inner


def local(orbitals, potential):
    previous = orbitals
    current = orbitals
    for degree_step in range(DEGREE):
        extended = with_halo(current, (("grid", 1),), 1)
        applied = apply_inner(extended, potential)
        if degree_step == 0:
            following = (applied - 5.0 * current) / 3.0
        else:
            following = 2.0 * (applied - 5.0 * current) / 3.0 - previous
        previous = current
        current = following
    count, zplanes, width = orbitals.shape
    filtered = current.astype(jnp.bfloat16).reshape(count, zplanes * width)
    pieces = lax.all_to_all(filtered, "band", split_axis=1, concat_axis=0, tiled=True)
    total_cells = pieces.shape[1] * lax.axis_size("band") * lax.axis_size("grid")
    partial_value = (
        lax.dot_general(
            pieces, pieces, (((1,), (1,)), ((), ())), preferred_element_type=jnp.float32
        )
        / total_cells
    )
    gram = lax.psum(partial_value, ("band", "grid"))
    scale = jnp.max(jnp.sum(jnp.abs(gram), axis=1))
    identity_mat = jnp.eye(gram.shape[0], dtype=jnp.float32)
    upper = gram / scale
    lower = identity_mat
    for sweep in range(NS_ITERS):
        factor = 1.5 * identity_mat - 0.5 * jnp.dot(lower, upper, precision=lax.Precision.HIGHEST)
        upper = jnp.dot(upper, factor, precision=lax.Precision.HIGHEST)
        lower = jnp.dot(factor, lower, precision=lax.Precision.HIGHEST)
    root = (lower / jnp.sqrt(scale)).astype(jnp.bfloat16)
    turned = lax.dot_general(
        root, pieces, (((0,), (0,)), ((), ())), preferred_element_type=jnp.float32
    )
    turned = turned.astype(jnp.bfloat16)
    returned = lax.all_to_all(turned, "band", split_axis=0, concat_axis=1, tiled=True)
    return returned.reshape(count, zplanes, width)


def solution(mesh):
    placed = (P("band", "grid", None), P("grid", None))
    return jax.shard_map(
        local, mesh=mesh, in_specs=placed, out_specs=P("band", "grid", None), check_vma=False
    )
```

profile of v0, /device:TPU:0, one launch (start us, length us, event | category | flops | bytes accessed | tf_op | source)
XLA Modules:
  0.0 102.4 jit_solution(3121627851999156750)
XLA Ops:
  0.0 0.0 copy-start
  0.0 1.9 %fusion.24 = (f32[16,1,4096]{2,1,0:T(1,128)S(1)}, f32[16,1,4096]{2,1,0:T(1,128)S(1)}) fusion(f32[16,2,4096]{2,1,0:T(2,128)} %param.2), kind=kLoop, calls=%fused_computation.42 | loop fusion | bytes 1048576 | tf_op jit(solution)/shard_map/slice | solution.py:20
  1.9 6.1 %collective-permute-start = (f32[16,1,4096]{2,1,0:T(1,128)S(1)}, f32[16,1,4096]{2,1,0:T(1,128)S(1)}, u32[]{:S(2)}, u32[]{:S(2)}) collective-permute-start(f32[16,1,4096]{2,1,0:T(1,128)S(1)} %get-tuple-element.25), channel_id=1, source_target_pairs={{1,0},{2,1},{3,2},{4,3},{5,4},{6,5},{7,6},{0,7},{9,8},{10,9},{11,1... | collective-permute-start | bytes 786440 | tf_op jit(solution)/shard_map/ppermute | solution.py:20
  7.9 0.0 collective-permute-start.1
  7.9 0.0 copy-done
  7.9 0.6 reshape.35
  8.6 0.4 fusion.19
  8.9 0.4 fusion.20
  9.3 0.0 copy-start.1
  9.3 0.2 fusion.21
  9.5 0.5 copy-done.1
  10.1 0.9 fusion.4
  11.0 0.5 add.58
  11.5 2.0 %collective-permute-done = f32[16,1,4096]{2,1,0:T(1,128)S(1)} collective-permute-done((f32[16,1,4096]{2,1,0:T(1,128)S(1)}, f32[16,1,4096]{2,1,0:T(1,128)S(1)}, u32[]{:S(2)}, u32[]{:S(2)}) %collective-permute-start) | collective-permute-done | bytes 262176 | tf_op jit(solution)/shard_map/ppermute | solution.py:20
  13.5 5.0 %collective-permute-done.1 = f32[16,1,4096]{2,1,0:T(1,128)} collective-permute-done((f32[16,1,4096]{2,1,0:T(1,128)S(1)}, f32[16,1,4096]{2,1,0:T(1,128)}, u32[]{:S(2)}, u32[]{:S(2)}) %collective-permute-start.1) | collective-permute-done | bytes 262176 | tf_op jit(solution)/shard_map/ppermute | solution.py:17
  18.5 2.4 %broadcast_multiply_fusion = (f32[16,2,4096]{2,1,0:T(2,128)S(1)}, f32[16,2,4096]{2,1,0:T(2,128)S(1)}) fusion(f32[16,2,4096]{2,1,0:T(2,128)S(1)} %copy-done, f32[2,4096]{1,0:T(2,128)S(1)} %copy-done.1, f32[16,2,4096]{2,1,0:T(2,128)S(1)} %add.58, f32[16,1,4096]{2,1,0:T(1,128)} %collective-permute-done.1, f32[16,1,4096]{2,1,0:T(1,128)S(1)} %collective-permute-done), kind=kLoop, calls=%fused_computation.26 | loop fusion | flops 1572864 | bytes 2654208 | tf_op jit(solution)/shard_map/div | solution.py:43
  21.0 0.6 reshape.36
  21.6 0.4 fusion.16
  22.0 0.2 fusion.17
  22.2 0.4 fusion.15
  22.5 1.3 %fusion.23 = (f32[16,1,4096]{2,1,0:T(1,128)}, f32[16,1,4096]{2,1,0:T(1,128)}) fusion(f32[16,2,4096]{2,1,0:T(2,128)S(1)} %get-tuple-element.5), kind=kLoop, calls=%fused_computation.41 | loop fusion | bytes 1048576 | tf_op jit(solution)/shard_map/slice | solution.py:20
  23.9 3.5 %collective-permute-start.2 = (f32[16,1,4096]{2,1,0:T(1,128)}, f32[16,1,4096]{2,1,0:T(1,128)S(1)}, u32[]{:S(2)}, u32[]{:S(2)}) collective-permute-start(f32[16,1,4096]{2,1,0:T(1,128)} %get-tuple-element.23), channel_id=1, source_target_pairs={{1,0},{2,1},{3,2},{4,3},{5,4},{6,5},{7,6},{0,7},{9,8},{10,9},{11,1... | collective-permute-start | bytes 786440 | tf_op jit(solution)/shard_map/ppermute | solution.py:20
  27.3 0.0 collective-permute-start.3
  27.4 0.9 fusion.6
  28.2 0.5 add.65
  28.8 8.5 %collective-permute-done.2 = f32[16,1,4096]{2,1,0:T(1,128)S(1)} collective-permute-done((f32[16,1,4096]{2,1,0:T(1,128)}, f32[16,1,4096]{2,1,0:T(1,128)S(1)}, u32[]{:S(2)}, u32[]{:S(2)}) %collective-permute-start.2) | collective-permute-done | bytes 262176 | tf_op jit(solution)/shard_map/ppermute | solution.py:20
  37.2 0.3 collective-permute-done.3
  37.5 2.6 %subtract_convert_fusion = bf16[16,2,4096]{2,1,0:T(2,128)(2,1)S(1)} fusion(f32[16,2,4096]{2,1,0:T(2,128)S(1)} %copy-done, f32[16,2,4096]{2,1,0:T(2,128)S(1)} %get-tuple-element.6, f32[16,2,4096]{2,1,0:T(2,128)S(1)} %add.65, f32[16,2,4096]{2,1,0:T(2,128)S(1)} %get-tuple-element.5, f32[16,1,4096]{2,1,0:T(1,128)} %collective-permute-done.3, ...), kind=kLoop, calls=%fused_computation.24 | loop fusion | flops 1835008 | bytes 2916352 | tf_op jit(solution)/shard_map/convert_element_type | solution.py:49
  40.1 0.1 all_to_all.26
  40.2 0.2 copy.7
  40.3 8.6 %all_to_all.35 = bf16[16,4,2048]{2,0,1:T(8,128)(2,1)S(1)} all-to-all(bf16[16,4,2048]{2,0,1:T(8,128)(2,1)S(1)} %copy.7), channel_id=1, replica_groups=mesh['band'=4,'grid'=8] {'band'}, dimensions={1} | all-to-all | bytes 524288 | tf_op jit(solution)/shard_map/all_to_all | solution.py:50
  48.9 0.2 convolution_multiply_fusion.2
  49.1 39.0 %psum.7 = f32[64,64]{1,0:T(8,128)S(1)} all-reduce(f32[64,64]{1,0:T(8,128)S(1)} %convolution_multiply_fusion.2), channel_id=1, replica_groups=mesh['band'=4,'grid'=8] {'band','grid'}, use_global_device_ids=true, to_apply=%region_0.1 | all-reduce | flops 4096 | bytes 32768 | tf_op jit(solution)/shard_map/psum | solution.py:58
  88.1 0.1 abs_reduce_fusion
  88.2 0.6 reduce_max.9
  88.8 0.8 fusion.1
  89.6 0.8 fusion.14
  90.4 0.1 fusion.13
  91.3 0.2 fusion
  91.5 0.2 fusion.2
  91.6 0.2 convolution_convert_fusion
  91.9 9.4 %all_to_all.36 = bf16[4,16,2048]{2,1,0:T(8,128)(2,1)S(1)} all-to-all(bf16[4,16,2048]{2,1,0:T(8,128)(2,1)S(1)} %bitcast.21), channel_id=1, replica_groups=mesh['band'=4,'grid'=8] {'band'}, dimensions={0} | all-to-all | bytes 524288 | tf_op jit(solution)/shard_map/all_to_all | solution.py:72
  101.2 0.2 copy.8
  101.5 0.9 reshape.37
  (3 shorter events, 0.1 us)
Async XLA Ops:
  0.0 7.9 %copy-start = (f32[16,2,4096]{2,1,0:T(2,128)S(1)}, f32[16,2,4096]{2,1,0:T(2,128)}, u32[]{:S(2)}) copy-start(f32[16,2,4096]{2,1,0:T(2,128)} %param.2) | copy-start | bytes 1572868
  1.9 11.6 %collective-permute-start = (f32[16,1,4096]{2,1,0:T(1,128)S(1)}, f32[16,1,4096]{2,1,0:T(1,128)S(1)}, u32[]{:S(2)}, u32[]{:S(2)}) collective-permute-start(f32[16,1,4096]{2,1,0:T(1,128)S(1)} %get-tuple-element.25), channel_id=1, source_target_pairs={{1,0},{2,1},{3,2},{4,3},{5,4},{6,5},{7,6},{0,7},{9,8},{10,9},{11,1... | collective-permute-start | bytes 786440 | tf_op jit(solution)/shard_map/ppermute | solution.py:20
  7.9 10.6 %collective-permute-start.1 = (f32[16,1,4096]{2,1,0:T(1,128)S(1)}, f32[16,1,4096]{2,1,0:T(1,128)}, u32[]{:S(2)}, u32[]{:S(2)}) collective-permute-start(f32[16,1,4096]{2,1,0:T(1,128)S(1)} %get-tuple-element.26), channel_id=1, source_target_pairs={{0,1},{1,2},{2,3},{3,4},{4,5},{5,6},{6,7},{7,0},{8,9},{9,10},{10,1... | collective-permute-start | bytes 786440 | tf_op jit(solution)/shard_map/ppermute | solution.py:17
  9.3 0.8 copy-start.1
  23.9 13.4 %collective-permute-start.2 = (f32[16,1,4096]{2,1,0:T(1,128)}, f32[16,1,4096]{2,1,0:T(1,128)S(1)}, u32[]{:S(2)}, u32[]{:S(2)}) collective-permute-start(f32[16,1,4096]{2,1,0:T(1,128)} %get-tuple-element.23), channel_id=1, source_target_pairs={{1,0},{2,1},{3,2},{4,3},{5,4},{6,5},{7,6},{0,7},{9,8},{10,9},{11,1... | collective-permute-start | bytes 786440 | tf_op jit(solution)/shard_map/ppermute | solution.py:20
  27.3 10.2 %collective-permute-start.3 = (f32[16,1,4096]{2,1,0:T(1,128)}, f32[16,1,4096]{2,1,0:T(1,128)}, u32[]{:S(2)}, u32[]{:S(2)}) collective-permute-start(f32[16,1,4096]{2,1,0:T(1,128)} %get-tuple-element.24), channel_id=1, source_target_pairs={{0,1},{1,2},{2,3},{3,4},{4,5},{5,6},{6,7},{7,0},{8,9},{9,10},{10,1... | collective-permute-start | bytes 786440 | tf_op jit(solution)/shard_map/ppermute | solution.py:17
where the time goes:
time: 103 us; the launch traced here: 102 us
  blocking collectives  56.9 us (55%)
  waiting for transfers between devices  15.7 us (15%)
  starting transfers between devices  9.52 us (9%)
  local copies, waits for them, and re-layouts  9.32 us (9%)
  other arithmetic  7.48 us (7%)
  matrix products  2.54 us (2%)
    psum x1, blocking collectives, local(): gram = lax.psum(partial_value, ('band', 'grid'))  39 us
    ppermute x2, waiting for transfers between devices, with_halo(): lax.ppermute(lax.slice_in_dim(block, 0, width, axis=dim), axis, backward)  10.5 us
    ppermute x2, starting transfers between devices, with_halo(): lax.ppermute(lax.slice_in_dim(block, 0, width, axis=dim), axis, backward)  9.51 us
    all_to_all x1, blocking collectives, local(): lax.all_to_all(turned, 'band', split_axis=0, concat_axis=1, tiled=True)  9.36 us
    all_to_all x1, blocking collectives, local(): lax.all_to_all(filtered, 'band', split_axis=1, concat_axis=0, tiled=True)  8.59 us
    ppermute x2, waiting for transfers between devices, with_halo(): lax.ppermute(lax.slice_in_dim(block, block.shape[dim] - width, None, axis...  5.27 us
    slice x2, local copies, waits for them, and re-layouts, with_halo(): lax.slice_in_dim(block, 0, width, axis=dim)  3.21 us
    convert_element_type x1, other arithmetic, local(): filtered = current.astype(jnp.bfloat16).reshape(count, zplanes * width)  2.58 us
  transfers between devices with their start and end apart: 4, of which 4 were waited for; matrix products, arithmetic and copies ran while one was open for 4% of the time, Pallas kernels for 0%

commit v1 on v0

--- a/solution.py
+++ b/solution.py
@@ -55,7 +55,7 @@
         )
         / total_cells
     )
-    gram = lax.psum(partial_value, ("band", "grid"))
+    gram = lax.psum(lax.psum(partial_value, "grid"), "band")
     scale = jnp.max(jnp.sum(jnp.abs(gram), axis=1))
     identity_mat = jnp.eye(gram.shape[0], dtype=jnp.float32)
     upper = gram / scale

time: 103 us -> 109 us (1.058)
  blocking collectives: 56.9 us -> 63.3 us
    psum x1 -> x2, blocking collectives: 39 us -> 46.3 us  [local(): gram = lax.psum(lax.psum(partial_value, 'grid'), 'band')]
where the time goes in v1:
time: 109 us
  blocking collectives  63.3 us (58%)
  waiting for transfers between devices  15.7 us (14%)
  starting transfers between devices  9.52 us (9%)
  local copies, waits for them, and re-layouts  9.32 us (9%)
  other arithmetic  7.48 us (7%)
  matrix products  2.54 us (2%)
    psum x2, blocking collectives, local(): gram = lax.psum(lax.psum(partial_value, 'grid'), 'band')  46.3 us
    ppermute x2, waiting for transfers between devices, with_halo(): lax.ppermute(lax.slice_in_dim(block, 0, width, axis=dim), axis, backward)  10.5 us
    ppermute x2, starting transfers between devices, with_halo(): lax.ppermute(lax.slice_in_dim(block, 0, width, axis=dim), axis, backward)  9.51 us
    all_to_all x1, blocking collectives, local(): lax.all_to_all(filtered, 'band', split_axis=1, concat_axis=0, tiled=True)  8.59 us
    all_to_all x1, blocking collectives, local(): lax.all_to_all(turned, 'band', split_axis=0, concat_axis=1, tiled=True)  8.39 us
    ppermute x2, waiting for transfers between devices, with_halo(): lax.ppermute(lax.slice_in_dim(block, block.shape[dim] - width, None, axis...  5.27 us
    slice x2, local copies, waits for them, and re-layouts, with_halo(): lax.slice_in_dim(block, 0, width, axis=dim)  3.22 us
    convert_element_type x1, other arithmetic, local(): filtered = current.astype(jnp.bfloat16).reshape(count, zplanes * width)  2.58 us
  transfers between devices with their start and end apart: 4, of which 4 were waited for; matrix products, arithmetic and copies ran while one was open for 4% of the time, Pallas kernels for 0%

profile of v1, /device:TPU:0, one launch (start us, length us, event | category | flops | bytes accessed | tf_op | source)
XLA Modules:
  0.0 108.8 jit_solution(18422071424940415079)
XLA Ops:
  0.0 0.0 copy-start
  0.0 1.9 %fusion.24 = (f32[16,1,4096]{2,1,0:T(1,128)S(1)}, f32[16,1,4096]{2,1,0:T(1,128)S(1)}) fusion(f32[16,2,4096]{2,1,0:T(2,128)} %param.2), kind=kLoop, calls=%fused_computation.42 | loop fusion | bytes 1048576 | tf_op jit(solution)/shard_map/slice | solution.py:20
  1.9 6.1 %collective-permute-start = (f32[16,1,4096]{2,1,0:T(1,128)S(1)}, f32[16,1,4096]{2,1,0:T(1,128)S(1)}, u32[]{:S(2)}, u32[]{:S(2)}) collective-permute-start(f32[16,1,4096]{2,1,0:T(1,128)S(1)} %get-tuple-element.25), channel_id=1, source_target_pairs={{1,0},{2,1},{3,2},{4,3},{5,4},{6,5},{7,6},{0,7},{9,8},{10,9},{11,1... | collective-permute-start | bytes 786440 | tf_op jit(solution)/shard_map/ppermute | solution.py:20
  7.9 0.0 collective-permute-start.1
  7.9 0.0 copy-done
  7.9 0.6 reshape.35
  8.6 0.4 fusion.19
  8.9 0.4 fusion.20
  9.3 0.0 copy-start.1
  9.3 0.2 fusion.21
  9.5 0.5 copy-done.1
  10.1 0.9 fusion.4
  11.0 0.5 add.60
  11.5 2.0 %collective-permute-done = f32[16,1,4096]{2,1,0:T(1,128)S(1)} collective-permute-done((f32[16,1,4096]{2,1,0:T(1,128)S(1)}, f32[16,1,4096]{2,1,0:T(1,128)S(1)}, u32[]{:S(2)}, u32[]{:S(2)}) %collective-permute-start) | collective-permute-done | bytes 262176 | tf_op jit(solution)/shard_map/ppermute | solution.py:20
  13.5 5.0 %collective-permute-done.1 = f32[16,1,4096]{2,1,0:T(1,128)} collective-permute-done((f32[16,1,4096]{2,1,0:T(1,128)S(1)}, f32[16,1,4096]{2,1,0:T(1,128)}, u32[]{:S(2)}, u32[]{:S(2)}) %collective-permute-start.1) | collective-permute-done | bytes 262176 | tf_op jit(solution)/shard_map/ppermute | solution.py:17
  18.5 2.4 %broadcast_multiply_fusion = (f32[16,2,4096]{2,1,0:T(2,128)S(1)}, f32[16,2,4096]{2,1,0:T(2,128)S(1)}) fusion(f32[16,2,4096]{2,1,0:T(2,128)S(1)} %copy-done, f32[2,4096]{1,0:T(2,128)S(1)} %copy-done.1, f32[16,2,4096]{2,1,0:T(2,128)S(1)} %add.60, f32[16,1,4096]{2,1,0:T(1,128)} %collective-permute-done.1, f32[16,1,4096]{2,1,0:T(1,128)S(1)} %collective-permute-done), kind=kLoop, calls=%fused_computation.26 | loop fusion | flops 1572864 | bytes 2654208 | tf_op jit(solution)/shard_map/div | solution.py:43
  21.0 0.6 reshape.36
  21.6 0.4 fusion.16
  22.0 0.2 fusion.17
  22.2 0.4 fusion.15
  22.5 1.3 %fusion.23 = (f32[16,1,4096]{2,1,0:T(1,128)}, f32[16,1,4096]{2,1,0:T(1,128)}) fusion(f32[16,2,4096]{2,1,0:T(2,128)S(1)} %get-tuple-element.5), kind=kLoop, calls=%fused_computation.41 | loop fusion | bytes 1048576 | tf_op jit(solution)/shard_map/slice | solution.py:20
  23.9 3.5 %collective-permute-start.2 = (f32[16,1,4096]{2,1,0:T(1,128)}, f32[16,1,4096]{2,1,0:T(1,128)S(1)}, u32[]{:S(2)}, u32[]{:S(2)}) collective-permute-start(f32[16,1,4096]{2,1,0:T(1,128)} %get-tuple-element.23), channel_id=1, source_target_pairs={{1,0},{2,1},{3,2},{4,3},{5,4},{6,5},{7,6},{0,7},{9,8},{10,9},{11,1... | collective-permute-start | bytes 786440 | tf_op jit(solution)/shard_map/ppermute | solution.py:20
  27.3 0.0 collective-permute-start.3
  27.4 0.9 fusion.6
  28.2 0.5 add.67
  28.8 8.5 %collective-permute-done.2 = f32[16,1,4096]{2,1,0:T(1,128)S(1)} collective-permute-done((f32[16,1,4096]{2,1,0:T(1,128)}, f32[16,1,4096]{2,1,0:T(1,128)S(1)}, u32[]{:S(2)}, u32[]{:S(2)}) %collective-permute-start.2) | collective-permute-done | bytes 262176 | tf_op jit(solution)/shard_map/ppermute | solution.py:20
  37.3 0.3 collective-permute-done.3
  37.5 2.6 %subtract_convert_fusion = bf16[16,2,4096]{2,1,0:T(2,128)(2,1)S(1)} fusion(f32[16,2,4096]{2,1,0:T(2,128)S(1)} %copy-done, f32[16,2,4096]{2,1,0:T(2,128)S(1)} %get-tuple-element.6, f32[16,2,4096]{2,1,0:T(2,128)S(1)} %add.67, f32[16,2,4096]{2,1,0:T(2,128)S(1)} %get-tuple-element.5, f32[16,1,4096]{2,1,0:T(1,128)} %collective-permute-done.3, ...), kind=kLoop, calls=%fused_computation.24 | loop fusion | flops 1835008 | bytes 2916352 | tf_op jit(solution)/shard_map/convert_element_type | solution.py:49
  40.1 0.1 all_to_all.26
  40.2 0.2 copy.7
  40.3 8.6 %all_to_all.35 = bf16[16,4,2048]{2,0,1:T(8,128)(2,1)S(1)} all-to-all(bf16[16,4,2048]{2,0,1:T(8,128)(2,1)S(1)} %copy.7), channel_id=1, replica_groups=mesh['band'=4,'grid'=8] {'band'}, dimensions={1} | all-to-all | bytes 524288 | tf_op jit(solution)/shard_map/all_to_all | solution.py:50
  48.9 0.2 convolution_multiply_fusion.2
  49.1 36.1 %psum.14 = f32[64,64]{1,0:T(8,128)S(1)} all-reduce(f32[64,64]{1,0:T(8,128)S(1)} %convolution_multiply_fusion.2), channel_id=1, replica_groups=mesh['band'=4,'grid'=8] {'grid'}, use_global_device_ids=true, to_apply=%region_0.1 | all-reduce | flops 4096 | bytes 32768 | tf_op jit(solution)/shard_map/psum | solution.py:58
  85.2 10.3 %psum.15 = f32[64,64]{1,0:T(8,128)S(1)} all-reduce(f32[64,64]{1,0:T(8,128)S(1)} %psum.14), channel_id=1, replica_groups=mesh['band'=4,'grid'=8] {'band'}, use_global_device_ids=true, to_apply=%region_1.2 | all-reduce | flops 4096 | bytes 32768 | tf_op jit(solution)/shard_map/psum | solution.py:58
  95.5 0.1 abs_reduce_fusion
  95.6 0.6 reduce_max.9
  96.2 0.8 fusion.1
  97.0 0.8 fusion.14
  97.8 0.1 fusion.13
  98.7 0.2 fusion
  98.8 0.2 fusion.2
  99.0 0.2 convolution_convert_fusion
  99.3 8.4 %all_to_all.36 = bf16[4,16,2048]{2,1,0:T(8,128)(2,1)S(1)} all-to-all(bf16[4,16,2048]{2,1,0:T(8,128)(2,1)S(1)} %bitcast.21), channel_id=1, replica_groups=mesh['band'=4,'grid'=8] {'band'}, dimensions={0} | all-to-all | bytes 524288 | tf_op jit(solution)/shard_map/all_to_all | solution.py:72
  107.6 0.2 copy.8
  107.9 0.9 reshape.37
  (3 shorter events, 0.1 us)
Async XLA Ops:
  0.0 7.9 %copy-start = (f32[16,2,4096]{2,1,0:T(2,128)S(1)}, f32[16,2,4096]{2,1,0:T(2,128)}, u32[]{:S(2)}) copy-start(f32[16,2,4096]{2,1,0:T(2,128)} %param.2) | copy-start | bytes 1572868
  1.9 11.6 %collective-permute-start = (f32[16,1,4096]{2,1,0:T(1,128)S(1)}, f32[16,1,4096]{2,1,0:T(1,128)S(1)}, u32[]{:S(2)}, u32[]{:S(2)}) collective-permute-start(f32[16,1,4096]{2,1,0:T(1,128)S(1)} %get-tuple-element.25), channel_id=1, source_target_pairs={{1,0},{2,1},{3,2},{4,3},{5,4},{6,5},{7,6},{0,7},{9,8},{10,9},{11,1... | collective-permute-start | bytes 786440 | tf_op jit(solution)/shard_map/ppermute | solution.py:20
  7.9 10.6 %collective-permute-start.1 = (f32[16,1,4096]{2,1,0:T(1,128)S(1)}, f32[16,1,4096]{2,1,0:T(1,128)}, u32[]{:S(2)}, u32[]{:S(2)}) collective-permute-start(f32[16,1,4096]{2,1,0:T(1,128)S(1)} %get-tuple-element.26), channel_id=1, source_target_pairs={{0,1},{1,2},{2,3},{3,4},{4,5},{5,6},{6,7},{7,0},{8,9},{9,10},{10,1... | collective-permute-start | bytes 786440 | tf_op jit(solution)/shard_map/ppermute | solution.py:17
  9.3 0.8 copy-start.1
  23.9 13.4 %collective-permute-start.2 = (f32[16,1,4096]{2,1,0:T(1,128)}, f32[16,1,4096]{2,1,0:T(1,128)S(1)}, u32[]{:S(2)}, u32[]{:S(2)}) collective-permute-start(f32[16,1,4096]{2,1,0:T(1,128)} %get-tuple-element.23), channel_id=1, source_target_pairs={{1,0},{2,1},{3,2},{4,3},{5,4},{6,5},{7,6},{0,7},{9,8},{10,9},{11,1... | collective-permute-start | bytes 786440 | tf_op jit(solution)/shard_map/ppermute | solution.py:20
  27.3 10.2 %collective-permute-start.3 = (f32[16,1,4096]{2,1,0:T(1,128)}, f32[16,1,4096]{2,1,0:T(1,128)}, u32[]{:S(2)}, u32[]{:S(2)}) collective-permute-start(f32[16,1,4096]{2,1,0:T(1,128)} %get-tuple-element.24), channel_id=1, source_target_pairs={{0,1},{1,2},{2,3},{3,4},{4,5},{5,6},{6,7},{7,0},{8,9},{9,10},{10,1... | collective-permute-start | bytes 786440 | tf_op jit(solution)/shard_map/ppermute | solution.py:17
